TPU v7x, 512 devices: a whole 4x4x16 slice. The times are simulated.
512 devices in a mesh: grp: 8 (over y, core), dev: 64 (over x, z).
Axes of the slice: x: 4, y: 4, z: 16, core: 2. Of those that a mesh axis runs over, the one named last changes fastest.
Arguments:
- offsets: float32 [2048, 3, 512], P(('grp', 'dev')), may hold values from 0 to 1
- sketch: bfloat16 [2048, 512, 256], P(('grp', 'dev')), may hold values from -6 to 6
- pattern: int32 [2048, 6], P(('grp', 'dev')), may hold values 0 or 1
- point_order: int32 [2048, 512], P(('grp', 'dev')), may hold values from 0 to 511, each once within a row
Outputs:
- basis: bfloat16 [2048, 512, 256], P(('grp', 'dev'))
- basis_factor: float32 [2048, 256, 256], P(('grp', 'dev'))
Inputs may be any that keep to these rules, and one draw needn't show every extreme that they name: `point_order`: each row is a permutation of 0 .. 511.
All inputs are finite; a program needn't handle non-finite values. No bound on the sum of `pattern` on one device may be relied on, other than what follows from the above.
Results may differ from a plain program's by a relative error of at most 0.0082.
Values may be sent and summed in bfloat16 or wider, within the bound.
A program may use at most 64 MiB of HBM per device.

v0:
```python
import math

import jax
import jax.numpy as jnp
from jax import lax
from jax.sharding import PartitionSpec as P

W = 4


wave_number = 40.0
decay_length = 4.0
softening = 0.5


def padded(block, sides, width):
    for axis, dim in sides:
        count = lax.axis_size(axis)
        forward = [(i, i + 1) for i in range(count - 1)]
        backward = [(target, source) for source, target in forward]
        low = lax.ppermute(
            lax.slice_in_dim(block, block.shape[dim] - width, None, axis=dim), axis, forward
        )
        high = lax.ppermute(lax.slice_in_dim(block, 0, width, axis=dim), axis, backward)
        block = jnp.concatenate([low, block, high], axis=dim)
    return block


def passed_along(array, axis, by):
    peers = lax.axis_size(axis)
    pairs = [(i, i + by) for i in range(peers) if 0 <= i + by < peers]
    return lax.ppermute(array, axis, pairs)


def offset_table(reach):
    return [-value for value in range(reach, 1, -1)] + list(range(2, reach + 1))


def with_index(points, start):
    count = points.shape[0]
    index = (start + jnp.arange(count, dtype=jnp.int32)).astype(points.dtype)
    unit = jnp.zeros((1, 3, 1), points.dtype).at[0, 0, 0].set(1.0)
    return points + index[:, None, None] * unit


def kernel_block(target_side, source_side, weight):
    squared = (target_side[0][:, None] - source_side[0][None, :]) ** 2
    squared = squared + (target_side[1][:, None] - source_side[1][None, :]) ** 2
    squared = squared + (target_side[2][:, None] - source_side[2][None, :]) ** 2
    distance = jnp.sqrt(squared)
    values = (
        jnp.cos(wave_number * distance) * jnp.exp(-distance / decay_length) / (distance + softening)
    )
    scale = weight * (1.0 / math.sqrt(target_side.shape[1]))
    return (values * scale).astype(jnp.bfloat16)


def basis_of(samples):
    gram = jnp.dot(
        samples.T, samples, precision=lax.Precision.HIGHEST, preferred_element_type=jnp.float32
    )
    width = gram.shape[0]
    shift = 0.01 * jnp.trace(gram) / width + 1e-05
    lower = jnp.linalg.cholesky(gram + shift * jnp.eye(width, dtype=jnp.float32))
    rows = jax.scipy.linalg.solve_triangular(lower, samples.T, lower=True)
    return (rows.T.astype(jnp.bfloat16), lower.T)


def body(offsets, sketch, pattern, point_order):
    count = offsets.shape[0]
    points = sketch.shape[1]
    width = sketch.shape[2]
    first_cluster = lax.axis_index(("grp", "dev")) * count
    places = with_index(offsets, first_cluster)
    order = jnp.broadcast_to(point_order[:, None, :], places.shape)
    targets = jnp.take_along_axis(places, order, axis=2)
    table = offset_table(W)
    window_targets = padded(targets, ((("grp", "dev"), 0),), W)
    window_pattern = padded(pattern, ((("grp", "dev"), 0),), W)
    partial_list = [jnp.zeros((points, width), jnp.float32) for slot in range(count + 2 * W)]
    for cluster in range(count):
        for column, shift_value in enumerate(table):
            slot = cluster + W - shift_value
            weight = window_pattern[slot, column].astype(jnp.float32)
            block = kernel_block(window_targets[slot], places[cluster], weight)
            partial_list[slot] = partial_list[slot] + jnp.dot(
                block, sketch[cluster], preferred_element_type=jnp.float32
            )
    lower_part = jnp.stack(partial_list[:W])
    upper_part = jnp.stack(partial_list[count + W :])
    own_part = jnp.stack(partial_list[W : W + count])
    from_lower = passed_along(upper_part, ("grp", "dev"), 1)
    from_upper = passed_along(lower_part, ("grp", "dev"), -1)
    filler = jnp.zeros((count - W, points, width), jnp.float32)
    samples = (
        own_part
        + jnp.concatenate([from_lower, filler], axis=0)
        + jnp.concatenate([filler, from_upper], axis=0)
    )
    basis, basis_factor = jax.vmap(basis_of)(samples)
    return (basis, basis_factor)


def solution(mesh):
    placed = (
        P(("grp", "dev"), None, None),
        P(("grp", "dev"), None, None),
        P(("grp", "dev"), None),
        P(("grp", "dev"), None),
    )
    return jax.shard_map(
        body,
        mesh=mesh,
        in_specs=placed,
        out_specs=(P(("grp", "dev"), None, None), P(("grp", "dev"), None, None)),
        check_vma=False,
    )
```

profile of v0, /device:TPU:24, one launch (start us, length us, event | category | flops | bytes accessed | tf_op | source)
XLA Modules:
  0.0 496.2 jit_solution(15473463164126830028)
XLA Ops:
  4.5 11.3 %collective-permute-start.1 = (s32[4,6]{1,0:T(4,128)}, s32[4,6]{1,0:T(4,128)S(1)}, u32[]{:S(2)}, u32[]{:S(2)}) collective-permute-start(s32[4,6]{1,0:T(4,128)} %param.8), channel_id=1, source_target_pairs={{1,0},{2,1},{3,2},{4,3},{5,4},{6,5},{7,6},{8,7},{9,8},{10,9},{11,1... | collective-permute-start | bytes 296 | tf_op jit(solution)/shard_map/ppermute | solution.py:24
  19.5 59.7 %gather_fusion = f32[6144]{0:T(1024)S(1)} fusion(f32[4,3,512]{2,0,1:T(4,128)S(1)} %broadcast_add_fusion, s32[6144]{0:T(1024)S(1)} %reshape.353), kind=kCustom, calls=%fused_computation | custom fusion | bytes 122880 | tf_op jit(solution)/shard_map/jit(take_along_axis)/gather | solution.py:76
  81.2 7.9 %collective-permute-start = (f32[4,3,512]{2,1,0:T(4,128)S(1)}, f32[4,3,512]{2,1,0:T(4,128)S(1)}, u32[]{:S(2)}, u32[]{:S(2)}) collective-permute-start(f32[4,3,512]{2,1,0:T(4,128)S(1)} %fusion.319), channel_id=1, source_target_pairs={{1,0},{2,1},{3,2},{4,3},{5,4},{6,5},{7,6},{8,7},{9,8},{10,9},{11,1... | collective-permute-start | bytes 73736 | tf_op jit(solution)/shard_map/ppermute | solution.py:24
  108.3 4.4 fusion.21
  112.8 4.5 convolution_add_fusion.3
  117.3 4.8 fusion.22
  122.1 4.5 convolution_add_fusion.1
  126.6 4.5 fusion.2
  131.1 4.7 fusion.20
  135.8 4.5 fusion.3
  140.3 5.2 %convolution_bitcast_fusion = f32[1,512,256]{2,1,0:T(8,128)S(1)} fusion(f32[]{:T(128)} %bitcast.66, f32[512]{0:T(512)S(1)} %bitcast.298, f32[512]{0:T(512)S(1)} %bitcast.299, f32[512]{0:T(512)S(1)} %bitcast.297, f32[512]{0:T(512)S(1)} %bitcast.263, f32[512]{0:T(512)S(1)} %bitcast.269, f32[512]{0:T(512)S(1)} %bitcast.257, bf16[4,512,256]{2,1,0:T(8,128)(2,1)S(1)} %copy-done.49), kind=kOutput, calls=%fused_computation.8 | convolution fusion | flops 138412032 | bytes 798724 | tf_op jit(solution)/shard_map/dot_general | solution.py:86
  145.5 4.5 fusion.1
  152.3 4.4 fusion.19
  156.8 4.5 fusion.4
  161.3 4.6 fusion.18
  166.0 4.5 convolution_add_fusion.7
  170.5 4.5 fusion.5
  175.1 4.8 fusion.17
  180.0 4.5 convolution_add_fusion.9
  184.5 4.7 fusion.6
  189.3 4.5 convolution_bitcast_fusion.1
  207.5 4.8 convolution_bitcast_fusion.3
  212.4 4.4 fusion.15
  216.8 4.5 fusion.7
  221.3 4.7 fusion.8
  226.0 21.0 %collective-permute-done.2 = f32[4,512,256]{2,1,0:T(8,128)S(1)} collective-permute-done((f32[4,512,256]{2,1,0:T(8,128)S(1)}, f32[4,512,256]{2,1,0:T(8,128)S(1)}, u32[]{:S(2)}, u32[]{:S(2)}) %collective-permute-start.2) | collective-permute-done | bytes 2097184 | tf_op jit(solution)/shard_map/ppermute | solution.py:32
  247.1 4.5 select_reduce_fusion
  255.5 47.1 %custom-call.17 = f32[4,128,128]{2,1,0:T(8,128)S(1)} custom-call(f32[4,128,128]{2,1,0:T(8,128)S(1)} %cholesky.119), custom_call_target="Cholesky" | custom-call | tf_op jit(solution)/shard_map/vmap(jit(cholesky))/cholesky | solution.py:64
  303.4 40.8 %custom-call.18 = f32[4,1,128,128]{2,3,1,0:T(8,128)} custom-call(f32[4,1,128,128]{3,2,1,0:T(8,128)} %select_bitcast_fusion), custom_call_target="InvertDiagBlocksLowerTriangular" | custom-call | tf_op jit(solution)/shard_map/vmap(jit(cholesky))/cholesky | solution.py:64
  347.9 48.4 %custom-call.19 = f32[4,128,128]{2,1,0:T(8,128)} custom-call(f32[4,128,128]{2,1,0:T(8,128)} %convolution_subtract_fusion), custom_call_target="Cholesky" | custom-call | tf_op jit(solution)/shard_map/vmap(jit(cholesky))/cholesky | solution.py:64
  400.8 5.4 %while.2 = (s32[]{:T(128)}, f32[4,256,256]{2,1,0:T(8,128)S(1)}, s32[2,2]{1,0:T(2,128)S(1)}, f32[2,4,128,128]{3,2,0,1:T(8,128)}, s32[]{:T(128)}) while((s32[]{:T(128)}, f32[4,256,256]{2,1,0:T(8,128)S(1)}, s32[2,2]{1,0:T(2,128)S(1)}, f32[2,4,128,128]{3,2,0,1:T(8,128)}, s32[]{:T(128)}) %tuple.102), condition=%wide.while_cond.1, body=%wide.while_body.1.sunk | while | flops 2 | bytes 525421 | solution.py:65
  406.2 80.3 %custom-call.20 = f32[4,2,128,128]{2,3,1,0:T(8,128)} custom-call(f32[4,2,128,128]{3,2,1,0:T(8,128)} %bitcast.339), custom_call_target="InvertDiagBlocksLowerTriangular" | custom-call | tf_op jit(solution)/shard_map/vmap(jit(_solve_triangular))/triangular_solve | solution.py:65
  (167 shorter events, 57.5 us)
Async XLA Ops:
  0.6 95.0 %collective-permute-start.4 = (s32[4,6]{1,0:T(4,128)}, s32[4,6]{1,0:T(4,128)S(1)}, u32[]{:S(2)}, u32[]{:S(2)}) collective-permute-start(s32[4,6]{1,0:T(4,128)} %param.8), channel_id=1, source_target_pairs={{0,1},{1,2},{2,3},{3,4},{4,5},{5,6},{6,7},{7,8},{8,9},{9,10},{10,1... | collective-permute-start | bytes 296 | tf_op jit(solution)/shard_map/ppermute | solution.py:21
  4.5 91.8 %collective-permute-start.1 = (s32[4,6]{1,0:T(4,128)}, s32[4,6]{1,0:T(4,128)S(1)}, u32[]{:S(2)}, u32[]{:S(2)}) collective-permute-start(s32[4,6]{1,0:T(4,128)} %param.8), channel_id=1, source_target_pairs={{1,0},{2,1},{3,2},{4,3},{5,4},{6,5},{7,6},{8,7},{9,8},{10,9},{11,1... | collective-permute-start | bytes 296 | tf_op jit(solution)/shard_map/ppermute | solution.py:24
  19.5 59.7 %copy-start.9 = (s32[4,512]{1,0:T(4,128)S(1)}, s32[4,512]{1,0:T(4,128)}, u32[]{:S(2)}) copy-start(s32[4,512]{1,0:T(4,128)} %param.9) | copy-start | bytes 24580
  19.5 69.6 %copy-start.11 = (s32[4,6]{1,0:T(4,128)S(1)}, s32[4,6]{1,0:T(4,128)}, u32[]{:S(2)}) copy-start(s32[4,6]{1,0:T(4,128)} %param.8) | copy-start | bytes 292
  19.5 88.8 %copy-start.49 = (bf16[4,512,256]{2,1,0:T(8,128)(2,1)S(1)}, bf16[4,512,256]{2,1,0:T(8,128)(2,1)}, u32[]{:S(2)}) copy-start(bf16[4,512,256]{2,1,0:T(8,128)(2,1)} %param.7) | copy-start | bytes 3145732
  79.2 29.1 %collective-permute-start.3 = (f32[4,3,512]{2,1,0:T(4,128)S(1)}, f32[4,3,512]{2,1,0:T(4,128)S(1)}, u32[]{:S(2)}, u32[]{:S(2)}) collective-permute-start(f32[4,3,512]{2,1,0:T(4,128)S(1)} %fusion.319), channel_id=1, source_target_pairs={{0,1},{1,2},{2,3},{3,4},{4,5},{5,6},{6,7},{7,8},{8,9},{9,10},{10,1... | collective-permute-start | bytes 73736 | tf_op jit(solution)/shard_map/ppermute | solution.py:21
  81.2 71.1 %collective-permute-start = (f32[4,3,512]{2,1,0:T(4,128)S(1)}, f32[4,3,512]{2,1,0:T(4,128)S(1)}, u32[]{:S(2)}, u32[]{:S(2)}) collective-permute-start(f32[4,3,512]{2,1,0:T(4,128)S(1)} %fusion.319), channel_id=1, source_target_pairs={{1,0},{2,1},{3,2},{4,3},{5,4},{6,5},{7,6},{8,7},{9,8},{10,9},{11,1... | collective-permute-start | bytes 73736 | tf_op jit(solution)/shard_map/ppermute | solution.py:24
  89.1 51.2 %copy-start.33 = (f32[1,1,512]{2,0,1:T(1,128)}, f32[1,1,512]{2,0,1:T(1,128)S(1)}, u32[]{:S(2)}) copy-start(f32[1,1,512]{2,0,1:T(1,128)S(1)} %get-tuple-element.79) | copy-start | bytes 6148
  89.1 51.2 %copy-start.35 = (f32[1,1,512]{2,0,1:T(1,128)}, f32[1,1,512]{2,0,1:T(1,128)S(1)}, u32[]{:S(2)}) copy-start(f32[1,1,512]{2,0,1:T(1,128)S(1)} %get-tuple-element.83) | copy-start | bytes 6148
  89.1 51.2 %copy-start.37 = (f32[1,1,512]{2,0,1:T(1,128)}, f32[1,1,512]{2,0,1:T(1,128)S(1)}, u32[]{:S(2)}) copy-start(f32[1,1,512]{2,0,1:T(1,128)S(1)} %get-tuple-element.84) | copy-start | bytes 6148
  89.1 67.6 %copy-start.12 = (f32[1,1,512]{2,0,1:T(1,128)}, f32[1,1,512]{2,0,1:T(1,128)S(1)}, u32[]{:S(2)}) copy-start(f32[1,1,512]{2,0,1:T(1,128)S(1)} %get-tuple-element.85) | copy-start | bytes 6148
  89.1 67.6 %copy-start.14 = (f32[1,1,512]{2,0,1:T(1,128)}, f32[1,1,512]{2,0,1:T(1,128)S(1)}, u32[]{:S(2)}) copy-start(f32[1,1,512]{2,0,1:T(1,128)S(1)} %get-tuple-element.86) | copy-start | bytes 6148
  89.1 67.6 %copy-start.16 = (f32[1,1,512]{2,0,1:T(1,128)}, f32[1,1,512]{2,0,1:T(1,128)S(1)}, u32[]{:S(2)}) copy-start(f32[1,1,512]{2,0,1:T(1,128)S(1)} %get-tuple-element.87) | copy-start | bytes 6148
  89.1 72.1 %copy-start.18 = (f32[1,1,512]{2,0,1:T(1,128)}, f32[1,1,512]{2,0,1:T(1,128)S(1)}, u32[]{:S(2)}) copy-start(f32[1,1,512]{2,0,1:T(1,128)S(1)} %get-tuple-element.80) | copy-start | bytes 6148
  89.2 72.1 %copy-start.20 = (f32[1,1,512]{2,0,1:T(1,128)}, f32[1,1,512]{2,0,1:T(1,128)S(1)}, u32[]{:S(2)}) copy-start(f32[1,1,512]{2,0,1:T(1,128)S(1)} %get-tuple-element.81) | copy-start | bytes 6148
  89.2 72.1 %copy-start.22 = (f32[1,1,512]{2,0,1:T(1,128)}, f32[1,1,512]{2,0,1:T(1,128)S(1)}, u32[]{:S(2)}) copy-start(f32[1,1,512]{2,0,1:T(1,128)S(1)} %get-tuple-element.82) | copy-start | bytes 6148
  89.2 76.7 %copy-start.24 = (f32[1,1,512]{2,0,1:T(1,128)}, f32[1,1,512]{2,0,1:T(1,128)S(1)}, u32[]{:S(2)}) copy-start(f32[1,1,512]{2,0,1:T(1,128)S(1)} %get-tuple-element.88) | copy-start | bytes 6148
  89.2 76.7 %copy-start.26 = (f32[1,1,512]{2,0,1:T(1,128)}, f32[1,1,512]{2,0,1:T(1,128)S(1)}, u32[]{:S(2)}) copy-start(f32[1,1,512]{2,0,1:T(1,128)S(1)} %get-tuple-element.89) | copy-start | bytes 6148
  89.2 76.8 %copy-start.28 = (f32[1,1,512]{2,0,1:T(1,128)}, f32[1,1,512]{2,0,1:T(1,128)S(1)}, u32[]{:S(2)}) copy-start(f32[1,1,512]{2,0,1:T(1,128)S(1)} %get-tuple-element.90) | copy-start | bytes 6148
  150.2 75.8 %collective-permute-start.5 = (f32[4,512,256]{2,1,0:T(8,128)S(1)}, f32[4,512,256]{2,1,0:T(8,128)S(1)}, u32[]{:S(2)}, u32[]{:S(2)}) collective-permute-start(f32[4,512,256]{2,1,0:T(8,128)S(1)} %pad_maximum_fusion.1), channel_id=1, source_target_pairs={{1,0},{2,1},{3,2},{4,3},{5,4},{6,5},{7,6},{8,7},{9,8},{10,9},{11,1... | collective-permute-start | bytes 6291464 | tf_op jit(solution)/shard_map/ppermute | solution.py:32
  175.1 4.9 copy-start.19
  175.1 4.9 copy-start.23
  193.9 53.1 %collective-permute-start.2 = (f32[4,512,256]{2,1,0:T(8,128)S(1)}, f32[4,512,256]{2,1,0:T(8,128)S(1)}, u32[]{:S(2)}, u32[]{:S(2)}) collective-permute-start(f32[4,512,256]{2,1,0:T(8,128)S(1)} %pad_maximum_fusion), channel_id=1, source_target_pairs={{0,1},{1,2},{2,3},{3,4},{4,5},{5,6},{6,7},{7,8},{8,9},{9,10},{10,1... | collective-permute-start | bytes 6291464 | tf_op jit(solution)/shard_map/ppermute | solution.py:32
  207.4 39.7 %copy-start.4 = (f32[1,512,256]{2,1,0:T(8,128)}, f32[1,512,256]{2,1,0:T(8,128)S(1)}, u32[]{:S(2)}) copy-start(f32[1,512,256]{2,1,0:T(8,128)S(1)} %convolution_bitcast_fusion.2) | copy-start | bytes 1572868
  207.5 4.9 copy-start.30
  207.5 4.9 copy-start.31
  207.5 4.9 copy-start.32
  212.3 34.7 %copy-start.5 = (f32[1,512,256]{2,1,0:T(8,128)}, f32[1,512,256]{2,1,0:T(8,128)S(1)}, u32[]{:S(2)}) copy-start(f32[1,512,256]{2,1,0:T(8,128)S(1)} %convolution_bitcast_fusion.3) | copy-start | bytes 1572868
  221.3 25.8 %copy-start.6 = (f32[1,512,256]{2,1,0:T(8,128)}, f32[1,512,256]{2,1,0:T(8,128)S(1)}, u32[]{:S(2)}) copy-start(f32[1,512,256]{2,1,0:T(8,128)S(1)} %fusion.7) | copy-start | bytes 1572868
  226.0 25.6 %copy-start.7 = (f32[1,512,256]{2,1,0:T(8,128)}, f32[1,512,256]{2,1,0:T(8,128)S(1)}, u32[]{:S(2)}) copy-start(f32[1,512,256]{2,1,0:T(8,128)S(1)} %fusion.8) | copy-start | bytes 1572868
  252.9 49.8 %copy-start.10 = (pred[128,128]{1,0:T(8,128)(4,1)S(1)}, pred[128,128]{1,0:T(8,128)(4,1)}, u32[]{:S(2)}) copy-start(pred[128,128]{1,0:T(8,128)(4,1)} %iota_compare_fusion.3) | copy-start | bytes 49156
  347.9 52.8 %copy-start.51 = (s32[2]{0:T(128)S(1)}, s32[2]{0:T(128)}, u32[]{:S(2)}) copy-start(s32[2]{0:T(128)} %iota_multiply_fusion) | copy-start | bytes 28
  (26 other events, 100.4 us)
where the time goes:
time: 506 us; the launch traced here: 496 us
  other arithmetic  231 us (46%)
  matrix products  122 us (24%)
  local copies, waits for them, and re-layouts  74.2 us (15%)
  starting transfers between devices  30.9 us (6%)
  waiting for transfers between devices  21.1 us (4%)
  between operations  16.9 us (3%)
    another operation x10, other arithmetic, basis_of(): jnp.linalg.cholesky(gram + shift * jnp.eye(width, dtype=jnp.float32))  139 us
    dot_general x24, matrix products, body(): jnp.dot(block, sketch[cluster], preferred_element_type=jnp.float32)  110 us
    another operation x3, other arithmetic, basis_of(): rows = jax.scipy.linalg.solve_triangular(lower, samples.T, lower=True)  80.8 us
    gather x3, local copies, waits for them, and re-layouts, body(): targets = jnp.take_along_axis(places, order, axis=2)  59.7 us
    ppermute x2, waiting for transfers between devices, passed_along(): return lax.ppermute(array, axis, pairs)  21.1 us
    ppermute x2, starting transfers between devices, padded(): lax.ppermute(lax.slice_in_dim(block, 0, width, axis=dim), axis, backward)  19.2 us
  transfers between devices with their start and end apart: 6, of which 1 were waited for; matrix products, arithmetic and copies ran while one was open for 36% of the time, Pallas kernels for 0%

commit v1 on v0

v1 whole, which is shorter than its diff:
```python
import math, functools
import numpy as np
import jax, jax.numpy as jnp
from jax import lax
from jax.experimental import pallas as pl
from jax.experimental.pallas import tpu as pltpu
F32=jnp.float32; BF=jnp.bfloat16
M=512
def cos_coeffs(deg):
    n=4000
    t=np.cos((np.arange(n)+.5)*np.pi/n)
    z=0.125+0.125*t
    f=np.sqrt(z)
    c=np.polynomial.chebyshev.Chebyshev.fit(z,np.cos(2*np.pi*f),deg,domain=[0,0.25])
    p=c.convert(kind=np.polynomial.Polynomial,domain=[-1,1],window=[-1,1]).coef
    return [float(v) for v in p]
COS=cos_coeffs(5)
SCALE=1.0/math.sqrt(512)
def value(u):
    r=u*lax.rsqrt(u)
    y=r*(40.0/(2*math.pi))
    k=(y+12582912.0)-12582912.0
    f=y-k
    z=f*f
    p=COS[5]*SCALE
    for c in COS[4::-1]:
        p=p*z+c*SCALE
    h=jnp.exp2(r*(-0.25*math.log2(math.e))-jnp.log2(r+0.5))
    return p*h
def split3(x):
    h=x.astype(BF).astype(F32); m=(x-h).astype(BF).astype(F32); return h,m,x-h-m
def prep(off, c, t_ref, s_ref):
    ax=(off[0:1]+c)-c
    n=ax*ax
    rows=[ax]
    for d in (1,2):
        v=off[d:d+1]; rows.append(v); n=n+v*v
    one=jnp.ones_like(ax); zero=jnp.zeros_like(ax)
    for d,v in enumerate(rows):
        h,m,l=split3(v)
        if t_ref is not None:
            for q,w in enumerate((h,h,m,m,h,l)): t_ref[6*d+q:6*d+q+1,:]=w
        if s_ref is not None:
            for q,w in enumerate((h,m,h,m,l,h)): s_ref[6*d+q:6*d+q+1,:]=-2.0*w
        if d==0: hx=(h,m,l)
    n3=split3(n)
    for q in range(3):
        if t_ref is not None:
            t_ref[18+q:19+q,:]=n3[q]; t_ref[21+q:22+q,:]=one; t_ref[24+q:25+q,:]=hx[q]; t_ref[27+q:28+q,:]=zero
        if s_ref is not None:
            s_ref[18+q:19+q,:]=one; s_ref[21+q:22+q,:]=n3[q]; s_ref[24+q:25+q,:]=zero; s_ref[27+q:28+q,:]=hx[q]
    if t_ref is not None:
        t_ref[30:31,:]=one; t_ref[31:32,:]=zero
    if s_ref is not None:
        s_ref[30:31,:]=zero; s_ref[31:32,:]=zero
def t_of(t, o):
    row=lax.broadcasted_iota(jnp.int32,t.shape,0)
    return (t+jnp.where((row>=27)&(row<30),2.0*o,0.0)).astype(BF)
def s_of(s, o):
    row=lax.broadcasted_iota(jnp.int32,s.shape,0)
    return (s+jnp.where((row>=24)&(row<27),-2.0*o,0.0)+jnp.where(row==30,o*o,0.0)).astype(BF)
from jax.sharding import PartitionSpec as P
MESH_ID=pl.DeviceIdType.MESH
CW=256
L_ORDER=(2,3,1,0); R_ORDER=(1,0,2,3)
def k1(groups, devs, count, off_ref, sk_ref, pat_ref, out_ref, hoff, own, hsk, tp, sp, so, ro, ss, rsem, loc):
    d=lax.axis_index("grp")*devs+lax.axis_index("dev")
    total=groups*devs
    right=lax.rem(d+1,total); left=lax.rem(d+total-1,total)
    rid=(right//devs,lax.rem(right,devs)); lid=(left//devs,lax.rem(left,devs))
    barrier=pltpu.get_barrier_semaphore()
    for n in (lid,rid):
        pl.semaphore_signal(barrier,inc=1,device_id=n,device_id_type=MESH_ID)
    local=pltpu.make_async_copy(sk_ref,own,loc)
    local.start()
    pl.semaphore_wait(barrier,2)
    def coff(side):
        return pltpu.make_async_remote_copy(off_ref,hoff.at[side],so.at[side],ro.at[side],device_id=rid if side==0 else lid,device_id_type=MESH_ID)
    def csk(side,j):
        return pltpu.make_async_remote_copy(sk_ref.at[j],hsk.at[side,j],ss.at[side,j],rsem.at[side,j],device_id=rid if side==0 else lid,device_id_type=MESH_ID)
    for side in (0,1): coff(side).start()
    for a,b in zip(L_ORDER,R_ORDER):
        csk(0,a).start(); csk(1,b).start()
    first=d*4
    ff=first.astype(F32)
    for s in range(4,8):
        prep(off_ref[s-4], ff+(s-4.0), tp.at[s-4], sp.at[s])
    out_ref[...]=jnp.zeros_like(out_ref)
    local.wait()
    def source(s,get):
        j=s-4
        tg=[i for i in range(4) if 2<=abs(j-i)<=4]
        i0,cnt=tg[0],len(tg)
        def body(t,_):
            i=i0+t
            oi=j-i; o=oi.astype(F32)
            k=jnp.where(oi<0,oi+4,oi+1)
            g=first+j
            w=jnp.where((g>=0)&(g<count),pat_ref[i,k],0).astype(F32)
            T=t_of(tp[i],o)
            acc=None
            for c in range(M//CW):
                S=s_of(sp[s,:,c*CW:(c+1)*CW],o)
                u=dot(T,S,0,0)
                kb=value(u).astype(BF)
                pr=dot(kb,get(c))
                acc=pr if acc is None else acc+pr
            out_ref[i]=out_ref[i]+w*acc
            return 0
        lax.fori_loop(0,cnt,body,0)
    def dot(a,b,ca=1,cb=0):
        return lax.dot_general(a,b,(((ca,),(cb,)),((),())),preferred_element_type=F32)
    for s in range(4,8):
        source(s,lambda c: own[s-4,c*CW:(c+1)*CW,:])
    for side in (0,1): coff(side).wait_recv()
    for s in range(4):
        prep(hoff[0,s], ff+(s-4.0), None, sp.at[s])
        prep(hoff[1,s], ff+(s+4.0), None, sp.at[8+s])
    for a,b in zip(L_ORDER,R_ORDER):
        csk(0,a).wait_recv()
        source(a,lambda c: hsk[0,a,c*CW:(c+1)*CW,:])
        csk(1,b).wait_recv()
        source(8+b,lambda c: hsk[1,b,c*CW:(c+1)*CW,:])
    for side in (0,1):
        coff(side).wait_send()
        for j in range(4): csk(side,j).wait_send()
def call1(mesh,offsets,sketch,pattern,count):
    g,dv=mesh.shape["grp"],mesh.shape["dev"]
    V=pl.BlockSpec(memory_space=pltpu.VMEM)
    return pl.pallas_call(functools.partial(k1,g,dv,count),out_shape=jax.ShapeDtypeStruct((4,512,256),F32),
      in_specs=[V,pl.BlockSpec(memory_space=pl.ANY),pl.BlockSpec(memory_space=pltpu.SMEM)],out_specs=V,
      scratch_shapes=[pltpu.VMEM((2,4,3,512),F32),pltpu.VMEM((4,512,256),BF),pltpu.VMEM((2,4,512,256),BF),
        pltpu.VMEM((4,32,512),F32),pltpu.VMEM((12,32,512),F32),
        pltpu.SemaphoreType.DMA((2,)),pltpu.SemaphoreType.DMA((2,)),pltpu.SemaphoreType.DMA((2,4)),pltpu.SemaphoreType.DMA((2,4)),pltpu.SemaphoreType.DMA],
      compiler_params=pltpu.CompilerParams(vmem_limit_bytes=50<<20,collective_id=0,has_side_effects=True))(offsets,sketch,pattern)
def cat3(xh,xl): pass
def hl(x):
    h=x.astype(BF); return h,(x-h.astype(F32)).astype(BF)
def dot(a,b,ca=1,cb=0):
    return lax.dot_general(a,b,(((ca,),(cb,)),((),())),preferred_element_type=F32)
NB=64; R=256; NC=4
def k2(s_ref, ord_ref, basis_ref, fac_ref, aug, xh, xl, xs):
    lane=lax.broadcasted_iota(jnp.int32,(NB,128),1)
    row=lax.broadcasted_iota(jnp.int32,(NB,128),0)
    r2=lax.broadcasted_iota(jnp.int32,(R,R),0); c2=lax.broadcasted_iota(jnp.int32,(R,R),1)
    eye=r2==c2
    for c in range(NC):
        st=s_ref[c].T
        aug[c,:,R:]=st
        th,tl=hl(st)
        g=dot(th,th,1,1)+(dot(th,tl,1,1)+dot(tl,th,1,1))
        tr=jnp.sum(jnp.where(eye,g,0.0),keepdims=True)
        shift=tr*(0.01/R)+1e-5
        aug[c,:,:R]=g+jnp.where(eye,shift,0.0)
    for jb in range(4):
        lt,half=jb//2,jb%2
        r0=jb*NB; rs=slice(r0,r0+NB); t0=lt*128; tile=slice(t0,t0+128)
        K=r0
        inA=(lane>=64) if half else (lane<64)
        other=(lane==row) if half else (lane==row+64)
        Ms=[]; lh=[None]*NC; ll=[None]*NC
        for c in range(NC):
            D=aug[c,rs,tile]
            if jb:
                lh[c]=xh[c,0:K,tile].T[64*half:64*half+64]
                ll[c]=xl[c,0:K,tile].T[64*half:64*half+64]
                bh,bl=xh[c,0:K,tile],xl[c,0:K,tile]
                D=D-(dot(lh[c],bh)+(dot(lh[c],bl)+dot(ll[c],bh)))
                aug[c,rs,tile]=D
            Mx=jnp.where(inA,D,jnp.where(other,1.0,0.0))
            Ms.append([Mx[8*g:8*g+8] for g in range(8)])
        rest=slice(t0+128,768)
        if jb:
            for c in range(NC):
                bh,bl=xh[c,0:K,rest],xl[c,0:K,rest]
                aug[c,rs,rest]=aug[c,rs,rest]-(dot(lh[c],bh)+(dot(lh[c],bl)+dot(ll[c],bh)))
        for j in range(NB):
            pj=64*half+j; g0,sj=j//8,j%8
            for c in range(NC):
                m=Ms[c]
                cb=[None]*8
                for g in range(g0,8):
                    cb[g]=jnp.broadcast_to(m[g][:,pj:pj+1],(8,128))
                rw=jnp.broadcast_to(m[g0][sj:sj+1,:],(8,128))
                pb=jnp.broadcast_to(cb[g0][sj:sj+1,:],(8,128))
                s=lax.rsqrt(pb)
                sc=rw*s
                xs[c,j:j+1,:]=sc[0:1]
                if j<NB-1:
                    q=sc*s
                    for g in range((j+1)//8,8):
                        m[g]=m[g]-cb[g]*q
        for c in range(NC):
            X=xs[c]
            U=jnp.where(inA&((lane-64*half)>=row),X,0.0)
            Li=X[:, 0:64] if half else X[:, 64:128]
            Lh,Ll=hl(Li)
            cols=slice(t0 if half==0 else t0+128,768)
            rh,rl=hl(aug[c,rs,cols])
            P=dot(Lh,rh)+(dot(Lh,rl)+dot(Ll,rh))
            ph,pl_=hl(P)
            xh[c,rs,cols]=ph; xl[c,rs,cols]=pl_
            if half==0:
                fac_ref[c,rs,tile]=jnp.where(inA,U,P[:,0:128])
                if lt==0: fac_ref[c,rs,128:256]=P[:,128:256]
            else:
                fac_ref[c,rs,tile]=U
                if lt==0: fac_ref[c,rs,128:256]=P[:,0:128]
            if lt==1: fac_ref[c,rs,0:128]=jnp.zeros((NB,128),F32)
    of=ord_ref[...].astype(F32)
    oT=jnp.concatenate([of,of],axis=0).T
    lane5=lax.broadcasted_iota(jnp.int32,(512,512),1).astype(F32)
    for c in range(NC):
        P=jnp.where(oT[:,c:c+1]==lane5,1.0,0.0).astype(BF)
        basis_ref[c]=dot(P,xh[c,:,R:],1,1).astype(BF)
def call2(samples,order,interpret=False):
    return pl.pallas_call(k2,out_shape=[jax.ShapeDtypeStruct((4,512,256),BF),jax.ShapeDtypeStruct((4,256,256),F32)],
      in_specs=[pl.BlockSpec(memory_space=pltpu.VMEM)]*2,out_specs=[pl.BlockSpec(memory_space=pltpu.VMEM)]*2,
      scratch_shapes=[pltpu.VMEM((4,256,768),F32),pltpu.VMEM((4,256,768),BF),pltpu.VMEM((4,256,768),BF),pltpu.VMEM((4,64,128),F32)],
      compiler_params=pltpu.CompilerParams(vmem_limit_bytes=50<<20))(samples,order)
def solution(mesh):
    placed=(P(("grp","dev"),None,None),P(("grp","dev"),None,None),P(("grp","dev"),None),P(("grp","dev"),None))
    devices=mesh.shape["grp"]*mesh.shape["dev"]
    def body(offsets,sketch,pattern,point_order):
        samples=call1(mesh,offsets,sketch,pattern,offsets.shape[0]*devices)
        return tuple(call2(samples,point_order))
    return jax.shard_map(body,mesh=mesh,in_specs=placed,out_specs=(P(("grp","dev"),None,None),P(("grp","dev"),None,None)),check_vma=False)
```

time: 506 us -> 88.4 us (0.17)
  the two profiles are of different devices: /device:TPU:24 before, /device:TPU:1 now
where the time goes in v1:
time: 88.4 us; the launch traced here: 88.2 us
  Pallas kernels  84.9 us (96%)
  local copies, waits for them, and re-layouts  2.66 us (3%)
    pallas_call x1, Pallas kernels, call1(): pl.pallas_call(functools.partial(k1, g, dv, count), out_shape=jax.ShapeDt...  44.1 us
    pallas_call x1, Pallas kernels, call2(): pl.pallas_call(k2, out_shape=[jax.ShapeDtypeStruct((4, 512, 256), BF), ja...  40.8 us
    unnamed x7, local copies, waits for them, and re-layouts  2.66 us

profile of v1, /device:TPU:1, one launch (start us, length us, event | category | flops | bytes accessed | tf_op | source)
XLA Modules:
  0.0 88.2 jit_solution(6155970856881284043)
XLA Ops:
  0.6 0.0 copy-start.1
  0.6 0.8 copy.6.off_ref
  1.4 0.0 copy-start
  1.4 1.2 %copy-done = bf16[4,512,256]{2,1,0:T(8,128)(2,1)S(1)} copy-done((bf16[4,512,256]{2,1,0:T(8,128)(2,1)S(1)}, bf16[4,512,256]{2,1,0:T(8,128)(2,1)}, u32[]{:S(2)}) %copy-start) | copy-done | bytes 1048600
  2.6 0.0 copy-start.2
  2.6 0.7 copy-done.2
  3.3 44.1 %shard_map.59.s_ref = f32[4,512,256]{2,1,0:T(8,128)S(1)} custom-call(f32[4,3,512]{2,1,0:T(4,128)S(1)} %copy.6.off_ref, bf16[4,512,256]{2,1,0:T(8,128)(2,1)S(1)} %copy-done, s32[4,6]{1,0:T(4,128)S(1)} %copy-done.2), custom_call_target="tpu_custom_call" | custom-call | tf_op jit(solution)/shard_map/pallas_call | solution.py:130
  47.4 0.0 copy-done.1
  47.4 40.8 %shard_map.60 = (bf16[4,512,256]{2,1,0:T(8,128)(2,1)}, f32[4,256,256]{2,1,0:T(8,128)}) custom-call(f32[4,512,256]{2,1,0:T(8,128)S(1)} %shard_map.59.s_ref, s32[4,512]{1,0:T(4,128)S(1)} %copy-done.1), custom_call_target="tpu_custom_call" | custom-call | tf_op jit(solution)/shard_map/pallas_call | solution.py:217
Async XLA Ops:
  0.6 46.8 %copy-start.1 = (s32[4,512]{1,0:T(4,128)S(1)}, s32[4,512]{1,0:T(4,128)}, u32[]{:S(2)}) copy-start(s32[4,512]{1,0:T(4,128)} %ord_ref.1) | copy-start | bytes 24580
  1.4 1.2 %copy-start = (bf16[4,512,256]{2,1,0:T(8,128)(2,1)S(1)}, bf16[4,512,256]{2,1,0:T(8,128)(2,1)}, u32[]{:S(2)}) copy-start(bf16[4,512,256]{2,1,0:T(8,128)(2,1)} %sk_ref.1) | copy-start | bytes 3145732
  2.6 0.7 copy-start.2

commit v2 on v1

v2 whole, which is shorter than its diff:
```python
import math, functools
import numpy as np
import jax, jax.numpy as jnp
from jax import lax
from jax.experimental import pallas as pl
from jax.experimental.pallas import tpu as pltpu
F32=jnp.float32; BF=jnp.bfloat16
M=512
def cos_coeffs(deg):
    n=4000
    t=np.cos((np.arange(n)+.5)*np.pi/n)
    z=0.125+0.125*t
    f=np.sqrt(z)
    c=np.polynomial.chebyshev.Chebyshev.fit(z,np.cos(2*np.pi*f),deg,domain=[0,0.25])
    p=c.convert(kind=np.polynomial.Polynomial,domain=[-1,1],window=[-1,1]).coef
    return [float(v) for v in p]
def sin_coeffs(deg):
    n=4000
    t=np.cos((np.arange(n)+.5)*np.pi/n)
    z=1/32+1/32*t
    g=np.sqrt(z)
    y=-np.sin(2*np.pi*g)/g
    w=np.sqrt(g)
    V=np.vander(z*16,deg+1,increasing=True)
    for _ in range(40):
        c=np.linalg.lstsq(V*(w*g)[:,None],y*w*g,rcond=None)[0]
        e=np.abs((V@c-y)*g)
        w=w*np.sqrt(1e-3+e/e.max()); w=w/w.max()
    return [float(v*16.0**n) for n,v in enumerate(c)]
SIN=sin_coeffs(3)
SIGMA=40.0/(2*math.pi)
SCALE=1.0/math.sqrt(512)
def value(u):
    y=u*lax.rsqrt(u)
    g=jnp.abs(y-jnp.round(y))-0.25
    z=g*g
    a=SCALE*SIGMA
    p=SIN[-1]*a
    for c in SIN[-2::-1]:
        p=p*z+c*a
    h=jnp.exp2(y*(-0.25*math.log2(math.e)/SIGMA)-jnp.log2(y+0.5*SIGMA))
    return (p*g)*h
def split3(x):
    h=x.astype(BF).astype(F32); m=(x-h).astype(BF).astype(F32); return h,m,x-h-m
def prep(off, c, t_ref, s_ref):
    x=jnp.concatenate([(off[0:1]+c)-c,off[1:3]],axis=0)
    if t_ref is not None:
        a=x*SIGMA
        n=a[0:1]*a[0:1]+a[1:2]*a[1:2]+a[2:3]*a[2:3]
        h,m,l=split3(a)
        for d in range(3):
            for q,w in enumerate((h,h,m,m,h,l)): t_ref[6*d+q:6*d+q+1,:]=w[d:d+1]
        one=jnp.ones_like(n)
        for q,w in enumerate(split3(n)):
            t_ref[18+q:19+q,:]=w; t_ref[21+q:22+q,:]=one
        t_ref[24:32,:]=jnp.zeros((8,x.shape[1]),F32)
    s_ref[0:3,:]=x
def s_rows(x, o, s_ref):
    b=jnp.concatenate([x[0:1]+o,x[1:3]],axis=0)*SIGMA
    n=b[0:1]*b[0:1]+b[1:2]*b[1:2]+b[2:3]*b[2:3]
    h,m,l=[-2.0*w for w in split3(b)]
    for d in range(3):
        for q,w in enumerate((h,m,h,m,l,h)): s_ref[6*d+q:6*d+q+1,:]=w[d:d+1]
    one=jnp.ones_like(n)
    for q,w in enumerate(split3(n)):
        s_ref[18+q:19+q,:]=one; s_ref[21+q:22+q,:]=w
    s_ref[24:32,:]=jnp.zeros((8,x.shape[1]),F32)
from jax.sharding import PartitionSpec as P
MESH_ID=pl.DeviceIdType.MESH
CHR=128
L_ORDER=(2,3,1,0); R_ORDER=(1,0,2,3)
def pair_list():
    order=[4,5,6,7]
    for a,b in zip(L_ORDER,R_ORDER): order+=[a,8+b]
    return [(s,i) for s in order for i in range(4) if 2<=abs(s-4-i)<=4]
PAIRS=pair_list()
def lookup(t,table):
    v=jnp.int32(table[0])
    for n in range(1,len(table)):
        if table[n]!=table[n-1]: v=jnp.where(t>=n,table[n],v)
    return v
def dot(a,b,ca=1,cb=0):
    return lax.dot_general(a,b,(((ca,),(cb,)),((),())),preferred_element_type=F32)
def stages(sk, tp, sp, sr, pat_ref, out_ref, u_ref, k_ref, first, count, CHR):
    def decode(t):
        t=jnp.clip(t,0,len(PAIRS)-1)
        return lookup(t,[p[0] for p in PAIRS]),lookup(t,[p[1] for p in PAIRS])
    def loadA(t):
        s,i=decode(t)
        o=(s-4-i).astype(F32)
        s_rows(sp[s],o,sr)
        return tp[i],sr[...].astype(BF)
    def Aval(ops,r):
        T,S=ops
        return dot(T[:,r*CHR:(r+1)*CHR],S,0,0)
    def A(ops,r):
        T,S=ops
        u_ref[r*CHR:(r+1)*CHR,:]=dot(T[:,r*CHR:(r+1)*CHR],S,0,0)
    def B(r):
        k_ref[r*CHR:(r+1)*CHR,:]=value(u_ref[r*CHR:(r+1)*CHR,:]).astype(BF)
    def infoC(t):
        s,i=decode(t)
        oi=s-4-i
        k=jnp.where(oi<0,oi+4,oi+1)
        g=first+s-4
        w=jnp.where((g>=0)&(g<count)&(t>=0),pat_ref[i,k],0).astype(F32)
        return s,i,w
    def C(info,r):
        s,i,w=info
        rows=slice(r*CHR,(r+1)*CHR)
        out_ref[i,rows,:]=out_ref[i,rows,:]+w*dot(k_ref[rows,:],sk[s])
    return loadA,A,B,infoC,C
def k1(groups, devs, count, off_ref, sk_ref, pat_ref, out_ref, hoff, sk, tf, tp, sp, sr, u_ref, k_ref, so, ro, ss, rsem, loc):
    d=lax.axis_index("grp")*devs+lax.axis_index("dev")
    total=groups*devs
    right=lax.rem(d+1,total); left=lax.rem(d+total-1,total)
    rid=(right//devs,lax.rem(right,devs)); lid=(left//devs,lax.rem(left,devs))
    barrier=pltpu.get_barrier_semaphore()
    for n in (lid,rid):
        pl.semaphore_signal(barrier,inc=1,device_id=n,device_id_type=MESH_ID)
    local=pltpu.make_async_copy(sk_ref,sk.at[4:8],loc)
    local.start()
    first=d*4
    ff=first.astype(F32)
    for s in range(4,8):
        prep(off_ref[s-4], ff+(s-4.0), tf, sp.at[s])
        tp[s-4]=tf[...].astype(BF)
    out_ref[...]=jnp.zeros_like(out_ref)
    k_ref[...]=jnp.zeros_like(k_ref)
    pl.semaphore_wait(barrier,2)
    def coff(side):
        return pltpu.make_async_remote_copy(off_ref,hoff.at[side],so.at[side],ro.at[side],device_id=rid if side==0 else lid,device_id_type=MESH_ID)
    def csk(side,j):
        return pltpu.make_async_remote_copy(sk_ref.at[j],sk.at[8*side+j],ss.at[side,j],rsem.at[side,j],device_id=rid if side==0 else lid,device_id_type=MESH_ID)
    for side in (0,1): coff(side).start()
    for a,b in zip(L_ORDER,R_ORDER):
        csk(0,a).start(); csk(1,b).start()
    loadA,A,B,infoC,C=stages(sk,tp,sp,sr,pat_ref,out_ref,u_ref,k_ref,first,count,CHR)
    N=M//CHR
    ops=loadA(jnp.int32(0))
    for r in range(N): A(ops,r)
    local.wait()
    def body(t,_):
        ops=loadA(t+1); info=infoC(t-1)
        for r in range(N):
            C(info,r); B(r); A(ops,r)
        return 0
    NLOC=6
    lax.fori_loop(0,NLOC-1,body,0)
    for side in (0,1): coff(side).wait_recv()
    for s in range(4):
        prep(hoff[0,s], ff+(s-4.0), None, sp.at[s])
        prep(hoff[1,s], ff+(s+4.0), None, sp.at[8+s])
    srcs=[p[0] for p in PAIRS]
    def wait_for(s):
        side,j=(0,s) if s<4 else (1,s-8)
        csk(side,j).wait_recv()
    def body2(t,_):
        for s in dict.fromkeys(srcs[NLOC:]):
            at=srcs.index(s)+1
            if at<len(PAIRS):
                @pl.when(t==at)
                def _(): wait_for(s)
        return body(t,_)
    lax.fori_loop(NLOC-1,len(PAIRS),body2,0)
    for s in dict.fromkeys(srcs[NLOC:]):
        if srcs.index(s)+1>=len(PAIRS): wait_for(s)
    info=infoC(jnp.int32(len(PAIRS)-1))
    for r in range(N): C(info,r)
    for side in (0,1):
        coff(side).wait_send()
        for j in range(4): csk(side,j).wait_send()
def call1(mesh,offsets,sketch,pattern,count):
    g,dv=mesh.shape["grp"],mesh.shape["dev"]
    V=pl.BlockSpec(memory_space=pltpu.VMEM)
    return pl.pallas_call(functools.partial(k1,g,dv,count),out_shape=jax.ShapeDtypeStruct((4,512,256),F32),
      in_specs=[V,pl.BlockSpec(memory_space=pl.ANY),pl.BlockSpec(memory_space=pltpu.SMEM)],out_specs=V,
      scratch_shapes=[pltpu.VMEM((2,4,3,512),F32),pltpu.VMEM((12,512,256),BF),
        pltpu.VMEM((32,512),F32),pltpu.VMEM((4,32,512),BF),pltpu.VMEM((12,3,512),F32),pltpu.VMEM((32,512),F32),
        pltpu.VMEM((512,512),F32),pltpu.VMEM((512,512),BF),
        pltpu.SemaphoreType.DMA((2,)),pltpu.SemaphoreType.DMA((2,)),pltpu.SemaphoreType.DMA((2,4)),pltpu.SemaphoreType.DMA((2,4)),pltpu.SemaphoreType.DMA],
      compiler_params=pltpu.CompilerParams(vmem_limit_bytes=50<<20,collective_id=0,has_side_effects=True))(offsets,sketch,pattern)
def cat3(xh,xl): pass
def hl(x):
    h=x.astype(BF); return h,(x-h.astype(F32)).astype(BF)
def dot(a,b,ca=1,cb=0):
    return lax.dot_general(a,b,(((ca,),(cb,)),((),())),preferred_element_type=F32)
NB=64; R=256; NC=4
def lanes(x,j):
    return jnp.take_along_axis(x,jnp.full((8,128),j,jnp.int32),axis=1,mode="promise_in_bounds")
def rows8(x,j):
    return jnp.broadcast_to(x[j:j+1,:],(8,128))
def k2(s_ref, ord_ref, basis_ref, fac_ref, aug, xh, xl, xs):
    lane=lax.broadcasted_iota(jnp.int32,(NB,128),1)
    row=lax.broadcasted_iota(jnp.int32,(NB,128),0)
    r2=lax.broadcasted_iota(jnp.int32,(R,R),0); c2=lax.broadcasted_iota(jnp.int32,(R,R),1)
    eye=r2==c2
    for c in range(NC):
        st=s_ref[c].T
        aug[c,:,R:]=st
        th,tl=hl(st)
        g=dot(th,th,1,1)+(dot(th,tl,1,1)+dot(tl,th,1,1))
        tr=jnp.sum(jnp.where(eye,g,0.0),keepdims=True)
        shift=tr*(0.01/R)+1e-5
        aug[c,:,:R]=g+jnp.where(eye,shift,0.0)
    sub8=lax.broadcasted_iota(jnp.int32,(8,128),0)
    for jb in range(4):
        lt,half=jb//2,jb%2
        r0=jb*NB; rs=slice(r0,r0+NB); t0=lt*128; tile=slice(t0,t0+128)
        K=r0
        inA=(lane>=64) if half else (lane<64)
        other=(lane==row) if half else (lane==row+64)
        Ms=[]; lh=[None]*NC; ll=[None]*NC
        for c in range(NC):
            D=aug[c,rs,tile]
            if jb:
                lh[c]=xh[c,0:K,tile].T[64*half:64*half+64]
                ll[c]=xl[c,0:K,tile].T[64*half:64*half+64]
                bh,bl=xh[c,0:K,tile],xl[c,0:K,tile]
                D=D-(dot(lh[c],bh)+(dot(lh[c],bl)+dot(ll[c],bh)))
                aug[c,rs,tile]=D
            Mx=jnp.where(inA,D,jnp.where(other,1.0,0.0))
            Ms.append([Mx[8*g:8*g+8] for g in range(8)])
        rest=slice(t0+128,768)
        if jb:
            for c in range(NC):
                bh,bl=xh[c,0:K,rest],xl[c,0:K,rest]
                aug[c,rs,rest]=aug[c,rs,rest]-(dot(lh[c],bh)+(dot(lh[c],bl)+dot(ll[c],bh)))
        for p in range(8):
            cb=[[None]*8 for _ in range(NC)]; col=[None]*NC; v=[None]*NC
            for g in range(p,8):
                for jj in range(8):
                    for c in range(NC):
                        b=lanes(Ms[c][g],64*half+8*p+jj)
                        if g==p: cb[c][jj]={}
                        cb[c][jj][g]=b
            for c in range(NC):
                col[c]=[cb[c][jj][p] for jj in range(8)]; v[c]=Ms[c][p]
            for jj in range(8):
                isj=sub8==jj
                for c in range(NC):
                    s=lax.rsqrt(rows8(col[c][jj],jj)); s2=s*s
                    rw=rows8(v[c],jj)
                    xs[c,8*p+jj:8*p+jj+1,:]=(rw*s)[0:1]
                    q=rw*s2
                    cj=col[c][jj]
                    v[c]=jnp.where(isj,q,v[c]-cj*q)
                    for kk in range(jj+1,8):
                        qk=rows8(col[c][kk],jj)*s2
                        col[c][kk]=jnp.where(isj,qk,col[c][kk]-cj*qk)
            for c in range(NC):
                w=[rows8(v[c],jj) for jj in range(8)]
                for g in range(p+1,8):
                    t=[cb[c][jj][g]*w[jj] for jj in range(8)]
                    while len(t)>1: t=[t[i]+t[i+1] for i in range(0,len(t),2)]
                    Ms[c][g]=Ms[c][g]-t[0]
        for c in range(NC):
            X=xs[c]
            U=jnp.where(inA&((lane-64*half)>=row),X,0.0)
            Li=X[:, 0:64] if half else X[:, 64:128]
            Lh,Ll=hl(Li)
            cols=slice(t0 if half==0 else t0+128,768)
            rh,rl=hl(aug[c,rs,cols])
            P=dot(Lh,rh)+(dot(Lh,rl)+dot(Ll,rh))
            ph,pl_=hl(P)
            xh[c,rs,cols]=ph; xl[c,rs,cols]=pl_
            if half==0:
                fac_ref[c,rs,tile]=jnp.where(inA,U,P[:,0:128])
                if lt==0: fac_ref[c,rs,128:256]=P[:,128:256]
            else:
                fac_ref[c,rs,tile]=U
                if lt==0: fac_ref[c,rs,128:256]=P[:,0:128]
            if lt==1: fac_ref[c,rs,0:128]=jnp.zeros((NB,128),F32)
    of=ord_ref[...].astype(F32)
    oT=jnp.concatenate([of,of],axis=0).T
    lane5=lax.broadcasted_iota(jnp.int32,(512,512),1).astype(F32)
    for c in range(NC):
        P=jnp.where(oT[:,c:c+1]==lane5,1.0,0.0).astype(BF)
        basis_ref[c]=dot(P,xh[c,:,R:],1,1).astype(BF)
def call2(samples,order,interpret=False):
    return pl.pallas_call(k2,out_shape=[jax.ShapeDtypeStruct((4,512,256),BF),jax.ShapeDtypeStruct((4,256,256),F32)],
      in_specs=[pl.BlockSpec(memory_space=pltpu.VMEM)]*2,out_specs=[pl.BlockSpec(memory_space=pltpu.VMEM)]*2,
      scratch_shapes=[pltpu.VMEM((4,256,768),F32),pltpu.VMEM((4,256,768),BF),pltpu.VMEM((4,256,768),BF),pltpu.VMEM((4,64,128),F32)],
      compiler_params=pltpu.CompilerParams(vmem_limit_bytes=50<<20))(samples,order)
def solution(mesh):
    placed=(P(("grp","dev"),None,None),P(("grp","dev"),None,None),P(("grp","dev"),None),P(("grp","dev"),None))
    devices=mesh.shape["grp"]*mesh.shape["dev"]
    def body(offsets,sketch,pattern,point_order):
        samples=call1(mesh,offsets,sketch,pattern,offsets.shape[0]*devices)
        return tuple(call2(samples,point_order))
    return jax.shard_map(body,mesh=mesh,in_specs=placed,out_specs=(P(("grp","dev"),None,None),P(("grp","dev"),None,None)),check_vma=False)
```

time: 88.4 us -> 57.9 us (0.65)
  Pallas kernels: 84.9 us -> 54.3 us
    pallas_call x1, Pallas kernels: 40.8 us -> 14.1 us  [call2(): pl.pallas_call(k2, out_shape=[jax.ShapeDtypeStruct((4, 512, 256), BF), ja...]
    pallas_call x1, Pallas kernels: 44.1 us -> 40.3 us  [call1(): pl.pallas_call(functools.partial(k1, g, dv, count), out_shape=jax.ShapeDt...]
where the time goes in v2:
time: 57.9 us; the launch traced here: 57.7 us
  Pallas kernels  54.3 us (94%)
  local copies, waits for them, and re-layouts  2.66 us (5%)
  between operations  0.67 us (1%)
    pallas_call x1, Pallas kernels, call1(): pl.pallas_call(functools.partial(k1, g, dv, count), out_shape=jax.ShapeDt...  40.3 us
    pallas_call x1, Pallas kernels, call2(): pl.pallas_call(k2, out_shape=[jax.ShapeDtypeStruct((4, 512, 256), BF), ja...  14.1 us
    unnamed x7, local copies, waits for them, and re-layouts  2.66 us

profile of v2, /device:TPU:1, one launch (start us, length us, event | category | flops | bytes accessed | tf_op | source)
XLA Modules:
  0.0 57.7 jit_solution(7827983870762669988)
XLA Ops:
  0.6 0.0 copy-start.1
  0.6 0.8 %copy.6.off_ref = f32[4,3,512]{2,1,0:T(4,128)S(1)} copy(f32[4,3,512]{2,0,1:T(4,128)} %param.4) | data formatting | bytes 49152 | tf_op args[0]
  1.4 0.0 copy-start
  1.4 1.2 %copy-done = bf16[4,512,256]{2,1,0:T(8,128)(2,1)S(1)} copy-done((bf16[4,512,256]{2,1,0:T(8,128)(2,1)S(1)}, bf16[4,512,256]{2,1,0:T(8,128)(2,1)}, u32[]{:S(2)}) %copy-start) | copy-done | bytes 1048600
  2.6 0.0 copy-start.2
  2.6 0.7 %copy-done.2 = s32[4,6]{1,0:T(4,128)S(1)} copy-done((s32[4,6]{1,0:T(4,128)S(1)}, s32[4,6]{1,0:T(4,128)}, u32[]{:S(2)}) %copy-start.2) | copy-done | bytes 120
  3.3 40.3 %shard_map.59.s_ref = f32[4,512,256]{2,1,0:T(8,128)S(1)} custom-call(f32[4,3,512]{2,1,0:T(4,128)S(1)} %copy.6.off_ref, bf16[4,512,256]{2,1,0:T(8,128)(2,1)S(1)} %copy-done, s32[4,6]{1,0:T(4,128)S(1)} %copy-done.2), custom_call_target="tpu_custom_call" | custom-call | tf_op jit(solution)/shard_map/pallas_call | solution.py:176
  43.6 0.0 copy-done.1
  43.6 14.1 %shard_map.60 = (bf16[4,512,256]{2,1,0:T(8,128)(2,1)}, f32[4,256,256]{2,1,0:T(8,128)}) custom-call(f32[4,512,256]{2,1,0:T(8,128)S(1)} %shard_map.59.s_ref, s32[4,512]{1,0:T(4,128)S(1)} %copy-done.1), custom_call_target="tpu_custom_call" | custom-call | tf_op jit(solution)/shard_map/pallas_call | solution.py:281
Async XLA Ops:
  0.6 43.0 %copy-start.1 = (s32[4,512]{1,0:T(4,128)S(1)}, s32[4,512]{1,0:T(4,128)}, u32[]{:S(2)}) copy-start(s32[4,512]{1,0:T(4,128)} %ord_ref.1) | copy-start | bytes 24580
  1.4 1.2 %copy-start = (bf16[4,512,256]{2,1,0:T(8,128)(2,1)S(1)}, bf16[4,512,256]{2,1,0:T(8,128)(2,1)}, u32[]{:S(2)}) copy-start(bf16[4,512,256]{2,1,0:T(8,128)(2,1)} %sk_ref.1) | copy-start | bytes 3145732
  2.6 0.7 %copy-start.2 = (s32[4,6]{1,0:T(4,128)S(1)}, s32[4,6]{1,0:T(4,128)}, u32[]{:S(2)}) copy-start(s32[4,6]{1,0:T(4,128)} %pat_ref.1) | copy-start | bytes 292

commit v3 on v2

--- a/solution.py
+++ b/solution.py
@@ -96,7 +96,7 @@
     def A(ops,r):
         T,S=ops
         u_ref[r*CHR:(r+1)*CHR,:]=dot(T[:,r*CHR:(r+1)*CHR],S,0,0)
-    def B(r):
+    def B(r,k_ref=k_ref):
         k_ref[r*CHR:(r+1)*CHR,:]=value(u_ref[r*CHR:(r+1)*CHR,:]).astype(BF)
     def infoC(t):
         s,i=decode(t)
@@ -105,12 +105,12 @@
         g=first+s-4
         w=jnp.where((g>=0)&(g<count)&(t>=0),pat_ref[i,k],0).astype(F32)
         return s,i,w
-    def C(info,r):
+    def C(info,r,k_ref=k_ref):
         s,i,w=info
         rows=slice(r*CHR,(r+1)*CHR)
         out_ref[i,rows,:]=out_ref[i,rows,:]+w*dot(k_ref[rows,:],sk[s])
     return loadA,A,B,infoC,C
-def k1(groups, devs, count, off_ref, sk_ref, pat_ref, out_ref, hoff, sk, tf, tp, sp, sr, u_ref, k_ref, so, ro, ss, rsem, loc):
+def k1(groups, devs, count, off_ref, sk_ref, pat_ref, ord_ref, out_ref, perm_ref, off, hoff, sk, pat, order, tf, tp, sp, sr, u_ref, k_ref, k2_ref, so, ro, ss, rsem, loc):
     d=lax.axis_index("grp")*devs+lax.axis_index("dev")
     total=groups*devs
     right=lax.rem(d+1,total); left=lax.rem(d+total-1,total)
@@ -118,68 +118,83 @@
     barrier=pltpu.get_barrier_semaphore()
     for n in (lid,rid):
         pl.semaphore_signal(barrier,inc=1,device_id=n,device_id_type=MESH_ID)
-    local=pltpu.make_async_copy(sk_ref,sk.at[4:8],loc)
-    local.start()
+    fetch=[pltpu.make_async_copy(a,b,loc.at[n]) for n,(a,b) in enumerate(((off_ref,off),(ord_ref,order),(pat_ref,pat),(sk_ref,sk.at[4:8])))]
+    for f in fetch: f.start()
     first=d*4
     ff=first.astype(F32)
-    for s in range(4,8):
-        prep(off_ref[s-4], ff+(s-4.0), tf, sp.at[s])
-        tp[s-4]=tf[...].astype(BF)
-    out_ref[...]=jnp.zeros_like(out_ref)
-    k_ref[...]=jnp.zeros_like(k_ref)
-    pl.semaphore_wait(barrier,2)
     def coff(side):
         return pltpu.make_async_remote_copy(off_ref,hoff.at[side],so.at[side],ro.at[side],device_id=rid if side==0 else lid,device_id_type=MESH_ID)
     def csk(side,j):
         return pltpu.make_async_remote_copy(sk_ref.at[j],sk.at[8*side+j],ss.at[side,j],rsem.at[side,j],device_id=rid if side==0 else lid,device_id_type=MESH_ID)
+    pl.semaphore_wait(barrier,2)
     for side in (0,1): coff(side).start()
     for a,b in zip(L_ORDER,R_ORDER):
         csk(0,a).start(); csk(1,b).start()
-    loadA,A,B,infoC,C=stages(sk,tp,sp,sr,pat_ref,out_ref,u_ref,k_ref,first,count,CHR)
+    fetch[0].wait()
+    for s in range(4,8):
+        prep(off[:,s-4,:], ff+(s-4.0), tf, sp.at[s])
+        tp[s-4]=tf[...].astype(BF)
+    fetch[1].wait()
+    of=order[...].astype(F32)
+    oT=jnp.concatenate([of,of],axis=0).T
+    lane5=lax.broadcasted_iota(jnp.int32,(M,M),1).astype(F32)
+    for c in range(4):
+        perm_ref[c]=jnp.where(oT[:,c:c+1]==lane5,1.0,0.0).astype(BF)
+    out_ref[...]=jnp.zeros_like(out_ref)
+    k_ref[...]=jnp.zeros_like(k_ref)
+    fetch[2].wait()
+    loadA,A,B,infoC,C=stages(sk,tp,sp,sr,pat,out_ref,u_ref,k_ref,first,count,CHR)
     N=M//CHR
     ops=loadA(jnp.int32(0))
     for r in range(N): A(ops,r)
-    local.wait()
+    fetch[3].wait()
     def body(t,_):
         ops=loadA(t+1); info=infoC(t-1)
         for r in range(N):
             C(info,r); B(r); A(ops,r)
         return 0
-    NLOC=6
+    NLOC=6; LAST=len(PAIRS)-1
     lax.fori_loop(0,NLOC-1,body,0)
     for side in (0,1): coff(side).wait_recv()
     for s in range(4):
-        prep(hoff[0,s], ff+(s-4.0), None, sp.at[s])
-        prep(hoff[1,s], ff+(s+4.0), None, sp.at[8+s])
+        prep(hoff[0,:,s,:], ff+(s-4.0), None, sp.at[s])
+        prep(hoff[1,:,s,:], ff+(s+4.0), None, sp.at[8+s])
     srcs=[p[0] for p in PAIRS]
     def wait_for(s):
         side,j=(0,s) if s<4 else (1,s-8)
         csk(side,j).wait_recv()
+    remote=list(dict.fromkeys(srcs[NLOC:]))
     def body2(t,_):
-        for s in dict.fromkeys(srcs[NLOC:]):
+        for s in remote:
             at=srcs.index(s)+1
-            if at<len(PAIRS):
+            if at<LAST:
                 @pl.when(t==at)
                 def _(): wait_for(s)
         return body(t,_)
-    lax.fori_loop(NLOC-1,len(PAIRS),body2,0)
-    for s in dict.fromkeys(srcs[NLOC:]):
-        if srcs.index(s)+1>=len(PAIRS): wait_for(s)
-    info=infoC(jnp.int32(len(PAIRS)-1))
+    lax.fori_loop(NLOC-1,LAST,body2,0)
+    for r in range(N): B(r,k2_ref)
+    for s in remote:
+        if srcs.index(s)+1==LAST: wait_for(s)
+    info=infoC(jnp.int32(LAST-1))
     for r in range(N): C(info,r)
+    for s in remote:
+        if srcs.index(s)==LAST: wait_for(s)
+    info=infoC(jnp.int32(LAST))
+    for r in range(N): C(info,r,k2_ref)
     for side in (0,1):
         coff(side).wait_send()
         for j in range(4): csk(side,j).wait_send()
-def call1(mesh,offsets,sketch,pattern,count):
+def call1(mesh,offsets,sketch,pattern,order,count):
     g,dv=mesh.shape["grp"],mesh.shape["dev"]
-    V=pl.BlockSpec(memory_space=pltpu.VMEM)
-    return pl.pallas_call(functools.partial(k1,g,dv,count),out_shape=jax.ShapeDtypeStruct((4,512,256),F32),
-      in_specs=[V,pl.BlockSpec(memory_space=pl.ANY),pl.BlockSpec(memory_space=pltpu.SMEM)],out_specs=V,
-      scratch_shapes=[pltpu.VMEM((2,4,3,512),F32),pltpu.VMEM((12,512,256),BF),
+    V=pl.BlockSpec(memory_space=pltpu.VMEM); H=pl.BlockSpec(memory_space=pltpu.HBM)
+    return pl.pallas_call(functools.partial(k1,g,dv,count),out_shape=[jax.ShapeDtypeStruct((4,512,256),F32),jax.ShapeDtypeStruct((4,512,512),BF)],
+      in_specs=[H,H,H,H],out_specs=[V,V],
+      scratch_shapes=[pltpu.VMEM((3,4,512),F32),pltpu.VMEM((2,3,4,512),F32),pltpu.VMEM((12,512,256),BF),
+        pltpu.SMEM((4,6),jnp.int32),pltpu.VMEM((4,512),jnp.int32),
         pltpu.VMEM((32,512),F32),pltpu.VMEM((4,32,512),BF),pltpu.VMEM((12,3,512),F32),pltpu.VMEM((32,512),F32),
-        pltpu.VMEM((512,512),F32),pltpu.VMEM((512,512),BF),
-        pltpu.SemaphoreType.DMA((2,)),pltpu.SemaphoreType.DMA((2,)),pltpu.SemaphoreType.DMA((2,4)),pltpu.SemaphoreType.DMA((2,4)),pltpu.SemaphoreType.DMA],
-      compiler_params=pltpu.CompilerParams(vmem_limit_bytes=50<<20,collective_id=0,has_side_effects=True))(offsets,sketch,pattern)
+        pltpu.VMEM((512,512),F32),pltpu.VMEM((512,512),BF),pltpu.VMEM((512,512),BF),
+        pltpu.SemaphoreType.DMA((2,)),pltpu.SemaphoreType.DMA((2,)),pltpu.SemaphoreType.DMA((2,4)),pltpu.SemaphoreType.DMA((2,4)),pltpu.SemaphoreType.DMA((4,))],
+      compiler_params=pltpu.CompilerParams(vmem_limit_bytes=40<<20,collective_id=0,has_side_effects=True))(*(pltpu.with_memory_space_constraint(x,pltpu.HBM) for x in (jnp.transpose(offsets,(1,0,2)),sketch,pattern,order)))
 def cat3(xh,xl): pass
 def hl(x):
     h=x.astype(BF); return h,(x-h.astype(F32)).astype(BF)
@@ -190,7 +205,12 @@
     return jnp.take_along_axis(x,jnp.full((8,128),j,jnp.int32),axis=1,mode="promise_in_bounds")
 def rows8(x,j):
     return jnp.broadcast_to(x[j:j+1,:],(8,128))
-def k2(s_ref, ord_ref, basis_ref, fac_ref, aug, xh, xl, xs):
+def k2(s_ref, perm_ref, basis_out, fac_out, basis_ref, fac_ref, aug, xh, xl, xs, bsem, fsem):
+    def fcopy(c,jb):
+        rows=pl.ds(jb*NB,NB)
+        return pltpu.make_async_copy(fac_ref.at[c,rows],fac_out.at[c,rows],fsem.at[c,jb])
+    def bcopy(c):
+        return pltpu.make_async_copy(basis_ref.at[c],basis_out.at[c],bsem.at[c])
     lane=lax.broadcasted_iota(jnp.int32,(NB,128),1)
     row=lax.broadcasted_iota(jnp.int32,(NB,128),0)
     r2=lax.broadcasted_iota(jnp.int32,(R,R),0); c2=lax.broadcasted_iota(jnp.int32,(R,R),1)
@@ -271,21 +291,24 @@
                 fac_ref[c,rs,tile]=U
                 if lt==0: fac_ref[c,rs,128:256]=P[:,0:128]
             if lt==1: fac_ref[c,rs,0:128]=jnp.zeros((NB,128),F32)
-    of=ord_ref[...].astype(F32)
-    oT=jnp.concatenate([of,of],axis=0).T
-    lane5=lax.broadcasted_iota(jnp.int32,(512,512),1).astype(F32)
+            fcopy(c,jb).start()
     for c in range(NC):
-        P=jnp.where(oT[:,c:c+1]==lane5,1.0,0.0).astype(BF)
-        basis_ref[c]=dot(P,xh[c,:,R:],1,1).astype(BF)
-def call2(samples,order,interpret=False):
+        basis_ref[c]=dot(perm_ref[c],xh[c,:,R:],1,1).astype(BF)
+        bcopy(c).start()
+    for c in range(NC):
+        for jb in range(4): fcopy(c,jb).wait()
+        bcopy(c).wait()
+def call2(samples,perm):
+    V=pl.BlockSpec(memory_space=pltpu.VMEM); H=pl.BlockSpec(memory_space=pltpu.HBM)
     return pl.pallas_call(k2,out_shape=[jax.ShapeDtypeStruct((4,512,256),BF),jax.ShapeDtypeStruct((4,256,256),F32)],
-      in_specs=[pl.BlockSpec(memory_space=pltpu.VMEM)]*2,out_specs=[pl.BlockSpec(memory_space=pltpu.VMEM)]*2,
-      scratch_shapes=[pltpu.VMEM((4,256,768),F32),pltpu.VMEM((4,256,768),BF),pltpu.VMEM((4,256,768),BF),pltpu.VMEM((4,64,128),F32)],
-      compiler_params=pltpu.CompilerParams(vmem_limit_bytes=50<<20))(samples,order)
+      in_specs=[V,V],out_specs=[H,H],
+      scratch_shapes=[pltpu.VMEM((4,512,256),BF),pltpu.VMEM((4,256,256),F32),pltpu.VMEM((4,256,768),F32),pltpu.VMEM((4,256,768),BF),pltpu.VMEM((4,256,768),BF),pltpu.VMEM((4,64,128),F32),
+        pltpu.SemaphoreType.DMA((4,)),pltpu.SemaphoreType.DMA((4,4))],
+      compiler_params=pltpu.CompilerParams(vmem_limit_bytes=40<<20))(samples,perm)
 def solution(mesh):
     placed=(P(("grp","dev"),None,None),P(("grp","dev"),None,None),P(("grp","dev"),None),P(("grp","dev"),None))
     devices=mesh.shape["grp"]*mesh.shape["dev"]
     def body(offsets,sketch,pattern,point_order):
-        samples=call1(mesh,offsets,sketch,pattern,offsets.shape[0]*devices)
-        return tuple(call2(samples,point_order))
+        samples,perm=call1(mesh,offsets,sketch,pattern,point_order,offsets.shape[0]*devices)
+        return tuple(call2(samples,perm))
     return jax.shard_map(body,mesh=mesh,in_specs=placed,out_specs=(P(("grp","dev"),None,None),P(("grp","dev"),None,None)),check_vma=False)

time: 57.9 us -> 54 us (0.933)
  local copies, waits for them, and re-layouts: 2.66 us -> 0 us
  Pallas kernels: 54.3 us -> 53 us
    unnamed x7 -> x0, local copies, waits for them, and re-layouts: 2.66 us -> none
    pallas_call x1, Pallas kernels: 40.3 us -> 39.3 us  [call1(): pl.pallas_call(functools.partial(k1, g, dv, count), out_shape=[jax.ShapeD...]
where the time goes in v3:
time: 54 us; the launch traced here: 53.8 us
  Pallas kernels  53 us (98%)
  between operations  0.8 us (1%)
    pallas_call x1, Pallas kernels, call1(): pl.pallas_call(functools.partial(k1, g, dv, count), out_shape=[jax.ShapeD...  39.3 us
    pallas_call x1, Pallas kernels, call2(): pl.pallas_call(k2, out_shape=[jax.ShapeDtypeStruct((4, 512, 256), BF), ja...  13.7 us

profile of v3, /device:TPU:1, one launch (start us, length us, event | category | flops | bytes accessed | tf_op | source)
XLA Modules:
  0.0 53.8 jit_solution(4815728136054081382)
XLA Ops:
  0.6 39.3 %shard_map.59 = (f32[4,512,256]{2,1,0:T(8,128)S(1)}, bf16[4,512,512]{2,1,0:T(8,128)(2,1)S(1)}) custom-call(f32[3,4,512]{2,1,0:T(4,128)} %bitcast.1, bf16[4,512,256]{2,1,0:T(8,128)(2,1)} %sk_ref.1, s32[4,6]{1,0:T(4,128)} %pat_ref.1, s32[4,512]{1,0:T(4,128)} %ord_ref.1), custom_call_target="tpu_custom_call" | custom-call | tf_op jit(solution)/shard_map/pallas_call | solution.py:190
  40.0 13.7 %shard_map.60 = (bf16[4,512,256]{2,1,0:T(8,128)(2,1)}, f32[4,256,256]{2,1,0:T(8,128)}) custom-call(f32[4,512,256]{2,1,0:T(8,128)S(1)} %get-tuple-element.4.s_ref, bf16[4,512,512]{2,1,0:T(8,128)(2,1)S(1)} %get-tuple-element.5.perm_ref), custom_call_target="tpu_custom_call" | custom-call | tf_op jit(solution)/shard_map/pallas_call | solution.py:303

commit v4 on v3

--- a/solution.py
+++ b/solution.py
@@ -70,9 +70,10 @@
 CHR=128
 L_ORDER=(2,3,1,0); R_ORDER=(1,0,2,3)
 def pair_list():
-    order=[4,5,6,7]
+    order=[]
     for a,b in zip(L_ORDER,R_ORDER): order+=[a,8+b]
-    return [(s,i) for s in order for i in range(4) if 2<=abs(s-4-i)<=4]
+    return LOCAL+[(s,i) for s in order for i in range(4) if 2<=abs(s-4-i)<=4]
+LOCAL=[(6,0),(7,0),(7,1)]
 PAIRS=pair_list()
 def lookup(t,table):
     v=jnp.int32(table[0])
@@ -109,8 +110,15 @@
         s,i,w=info
         rows=slice(r*CHR,(r+1)*CHR)
         out_ref[i,rows,:]=out_ref[i,rows,:]+w*dot(k_ref[rows,:],sk[s])
-    return loadA,A,B,infoC,C
-def k1(groups, devs, count, off_ref, sk_ref, pat_ref, ord_ref, out_ref, perm_ref, off, hoff, sk, pat, order, tf, tp, sp, sr, u_ref, k_ref, k2_ref, so, ro, ss, rsem, loc):
+    def D(t):
+        s,i=decode(t)
+        o=i-(s-4)
+        w=jnp.where(t>=0,pat_ref[s-4,jnp.where(o<0,o+4,o+1)],0).astype(F32)
+        for r in range(M//CHR):
+            rows=slice(r*CHR,(r+1)*CHR)
+            out_ref[s-4,rows,:]=out_ref[s-4,rows,:]+w*dot(k_ref[:,rows],sk[4+i],0,0)
+    return loadA,A,B,infoC,C,D
+def k1(groups, devs, count, off_ref, sk_ref, pat_ref, ord_ref, out_ref, perm_ref, mid_ref, off, hoff, sk, pat, order, tf, tp, sp, sr, u_ref, k_ref, k2_ref, so, ro, ss, rsem, loc):
     d=lax.axis_index("grp")*devs+lax.axis_index("dev")
     total=groups*devs
     right=lax.rem(d+1,total); left=lax.rem(d+total-1,total)
@@ -130,6 +138,8 @@
     for side in (0,1): coff(side).start()
     for a,b in zip(L_ORDER,R_ORDER):
         csk(0,a).start(); csk(1,b).start()
+    out_ref[...]=jnp.zeros_like(out_ref)
+    k_ref[...]=jnp.zeros_like(k_ref)
     fetch[0].wait()
     for s in range(4,8):
         prep(off[:,s-4,:], ff+(s-4.0), tf, sp.at[s])
@@ -140,10 +150,8 @@
     lane5=lax.broadcasted_iota(jnp.int32,(M,M),1).astype(F32)
     for c in range(4):
         perm_ref[c]=jnp.where(oT[:,c:c+1]==lane5,1.0,0.0).astype(BF)
-    out_ref[...]=jnp.zeros_like(out_ref)
-    k_ref[...]=jnp.zeros_like(k_ref)
     fetch[2].wait()
-    loadA,A,B,infoC,C=stages(sk,tp,sp,sr,pat,out_ref,u_ref,k_ref,first,count,CHR)
+    loadA,A,B,infoC,C,D=stages(sk,tp,sp,sr,pat,out_ref,u_ref,k_ref,first,count,CHR)
     N=M//CHR
     ops=loadA(jnp.int32(0))
     for r in range(N): A(ops,r)
@@ -153,8 +161,11 @@
         for r in range(N):
             C(info,r); B(r); A(ops,r)
         return 0
-    NLOC=6; LAST=len(PAIRS)-1
-    lax.fori_loop(0,NLOC-1,body,0)
+    def both(t,_):
+        D(t-1)
+        return body(t,_)
+    NLOC=len(LOCAL); LAST=len(PAIRS)-1
+    lax.fori_loop(0,NLOC-1,both,0)
     for side in (0,1): coff(side).wait_recv()
     for s in range(4):
         prep(hoff[0,:,s,:], ff+(s-4.0), None, sp.at[s])
@@ -171,8 +182,10 @@
                 @pl.when(t==at)
                 def _(): wait_for(s)
         return body(t,_)
-    lax.fori_loop(NLOC-1,LAST,body2,0)
+    lax.fori_loop(NLOC-1,NLOC+1,both,0)
+    lax.fori_loop(NLOC+1,LAST,body2,0)
     for r in range(N): B(r,k2_ref)
+    for c in (1,2): augment(out_ref[c],mid_ref.at[c-1])
     for s in remote:
         if srcs.index(s)+1==LAST: wait_for(s)
     info=infoC(jnp.int32(LAST-1))
@@ -187,8 +200,8 @@
 def call1(mesh,offsets,sketch,pattern,order,count):
     g,dv=mesh.shape["grp"],mesh.shape["dev"]
     V=pl.BlockSpec(memory_space=pltpu.VMEM); H=pl.BlockSpec(memory_space=pltpu.HBM)
-    return pl.pallas_call(functools.partial(k1,g,dv,count),out_shape=[jax.ShapeDtypeStruct((4,512,256),F32),jax.ShapeDtypeStruct((4,512,512),BF)],
-      in_specs=[H,H,H,H],out_specs=[V,V],
+    return pl.pallas_call(functools.partial(k1,g,dv,count),out_shape=[jax.ShapeDtypeStruct((4,512,256),F32),jax.ShapeDtypeStruct((4,512,512),BF),jax.ShapeDtypeStruct((2,256,768),F32)],
+      in_specs=[H,H,H,H],out_specs=[V,V,V],
       scratch_shapes=[pltpu.VMEM((3,4,512),F32),pltpu.VMEM((2,3,4,512),F32),pltpu.VMEM((12,512,256),BF),
         pltpu.SMEM((4,6),jnp.int32),pltpu.VMEM((4,512),jnp.int32),
         pltpu.VMEM((32,512),F32),pltpu.VMEM((4,32,512),BF),pltpu.VMEM((12,3,512),F32),pltpu.VMEM((32,512),F32),
@@ -205,7 +218,15 @@
     return jnp.take_along_axis(x,jnp.full((8,128),j,jnp.int32),axis=1,mode="promise_in_bounds")
 def rows8(x,j):
     return jnp.broadcast_to(x[j:j+1,:],(8,128))
-def k2(s_ref, perm_ref, basis_out, fac_out, basis_ref, fac_ref, aug, xh, xl, xs, bsem, fsem):
+def augment(samples,ref):
+    eye=lax.broadcasted_iota(jnp.int32,(R,R),0)==lax.broadcasted_iota(jnp.int32,(R,R),1)
+    st=samples.T
+    ref[:,R:]=st
+    th,tl=hl(st)
+    g=dot(th,th,1,1)+(dot(th,tl,1,1)+dot(tl,th,1,1))
+    tr=jnp.sum(jnp.where(eye,g,0.0),keepdims=True)
+    ref[:,:R]=g+jnp.where(eye,tr*(0.01/R)+1e-5,0.0)
+def k2(s_ref, perm_ref, mid_ref, basis_out, fac_out, basis_ref, fac_ref, aug, upd, xh, xl, xs, bsem, fsem):
     def fcopy(c,jb):
         rows=pl.ds(jb*NB,NB)
         return pltpu.make_async_copy(fac_ref.at[c,rows],fac_out.at[c,rows],fsem.at[c,jb])
@@ -213,16 +234,8 @@
         return pltpu.make_async_copy(basis_ref.at[c],basis_out.at[c],bsem.at[c])
     lane=lax.broadcasted_iota(jnp.int32,(NB,128),1)
     row=lax.broadcasted_iota(jnp.int32,(NB,128),0)
-    r2=lax.broadcasted_iota(jnp.int32,(R,R),0); c2=lax.broadcasted_iota(jnp.int32,(R,R),1)
-    eye=r2==c2
-    for c in range(NC):
-        st=s_ref[c].T
-        aug[c,:,R:]=st
-        th,tl=hl(st)
-        g=dot(th,th,1,1)+(dot(th,tl,1,1)+dot(tl,th,1,1))
-        tr=jnp.sum(jnp.where(eye,g,0.0),keepdims=True)
-        shift=tr*(0.01/R)+1e-5
-        aug[c,:,:R]=g+jnp.where(eye,shift,0.0)
+    src=[aug.at[0],mid_ref.at[0],mid_ref.at[1],aug.at[1]]
+    for c in (0,3): augment(s_ref[c],src[c])
     sub8=lax.broadcasted_iota(jnp.int32,(8,128),0)
     for jb in range(4):
         lt,half=jb//2,jb%2
@@ -232,20 +245,20 @@
         other=(lane==row) if half else (lane==row+64)
         Ms=[]; lh=[None]*NC; ll=[None]*NC
         for c in range(NC):
-            D=aug[c,rs,tile]
+            D=src[c][rs,tile]
             if jb:
                 lh[c]=xh[c,0:K,tile].T[64*half:64*half+64]
                 ll[c]=xl[c,0:K,tile].T[64*half:64*half+64]
                 bh,bl=xh[c,0:K,tile],xl[c,0:K,tile]
                 D=D-(dot(lh[c],bh)+(dot(lh[c],bl)+dot(ll[c],bh)))
-                aug[c,rs,tile]=D
+                upd[c,:,tile]=D
             Mx=jnp.where(inA,D,jnp.where(other,1.0,0.0))
             Ms.append([Mx[8*g:8*g+8] for g in range(8)])
         rest=slice(t0+128,768)
         if jb:
             for c in range(NC):
                 bh,bl=xh[c,0:K,rest],xl[c,0:K,rest]
-                aug[c,rs,rest]=aug[c,rs,rest]-(dot(lh[c],bh)+(dot(lh[c],bl)+dot(ll[c],bh)))
+                upd[c,:,rest]=src[c][rs,rest]-(dot(lh[c],bh)+(dot(lh[c],bl)+dot(ll[c],bh)))
         for p in range(8):
             cb=[[None]*8 for _ in range(NC)]; col=[None]*NC; v=[None]*NC
             for g in range(p,8):
@@ -280,7 +293,7 @@
             Li=X[:, 0:64] if half else X[:, 64:128]
             Lh,Ll=hl(Li)
             cols=slice(t0 if half==0 else t0+128,768)
-            rh,rl=hl(aug[c,rs,cols])
+            rh,rl=hl(upd[c,:,cols] if jb else src[c][rs,cols])
             P=dot(Lh,rh)+(dot(Lh,rl)+dot(Ll,rh))
             ph,pl_=hl(P)
             xh[c,rs,cols]=ph; xl[c,rs,cols]=pl_
@@ -298,17 +311,17 @@
     for c in range(NC):
         for jb in range(4): fcopy(c,jb).wait()
         bcopy(c).wait()
-def call2(samples,perm):
+def call2(samples,perm,mid):
     V=pl.BlockSpec(memory_space=pltpu.VMEM); H=pl.BlockSpec(memory_space=pltpu.HBM)
     return pl.pallas_call(k2,out_shape=[jax.ShapeDtypeStruct((4,512,256),BF),jax.ShapeDtypeStruct((4,256,256),F32)],
-      in_specs=[V,V],out_specs=[H,H],
-      scratch_shapes=[pltpu.VMEM((4,512,256),BF),pltpu.VMEM((4,256,256),F32),pltpu.VMEM((4,256,768),F32),pltpu.VMEM((4,256,768),BF),pltpu.VMEM((4,256,768),BF),pltpu.VMEM((4,64,128),F32),
+      in_specs=[V,V,V],out_specs=[H,H],
+      scratch_shapes=[pltpu.VMEM((4,512,256),BF),pltpu.VMEM((4,256,256),F32),pltpu.VMEM((2,256,768),F32),pltpu.VMEM((4,64,768),F32),pltpu.VMEM((4,256,768),BF),pltpu.VMEM((4,256,768),BF),pltpu.VMEM((4,64,128),F32),
         pltpu.SemaphoreType.DMA((4,)),pltpu.SemaphoreType.DMA((4,4))],
-      compiler_params=pltpu.CompilerParams(vmem_limit_bytes=40<<20))(samples,perm)
+      compiler_params=pltpu.CompilerParams(vmem_limit_bytes=40<<20))(samples,perm,mid)
 def solution(mesh):
     placed=(P(("grp","dev"),None,None),P(("grp","dev"),None,None),P(("grp","dev"),None),P(("grp","dev"),None))
     devices=mesh.shape["grp"]*mesh.shape["dev"]
     def body(offsets,sketch,pattern,point_order):
-        samples,perm=call1(mesh,offsets,sketch,pattern,point_order,offsets.shape[0]*devices)
-        return tuple(call2(samples,perm))
+        samples,perm,mid=call1(mesh,offsets,sketch,pattern,point_order,offsets.shape[0]*devices)
+        return tuple(call2(samples,perm,mid))
     return jax.shard_map(body,mesh=mesh,in_specs=placed,out_specs=(P(("grp","dev"),None,None),P(("grp","dev"),None,None)),check_vma=False)

time: 54 us -> 54.1 us (level)
    pallas_call x1, Pallas kernels: 39.3 us -> 40.1 us  [call1(): pl.pallas_call(functools.partial(k1, g, dv, count), out_shape=[jax.ShapeD...]
    pallas_call x1, Pallas kernels: 13.7 us -> 13.1 us  [call2(): pl.pallas_call(k2, out_shape=[jax.ShapeDtypeStruct((4, 512, 256), BF), ja...]
where the time goes in v4:
time: 54.1 us; the launch traced here: 54 us
  Pallas kernels  53.2 us (98%)
  between operations  0.8 us (1%)
    pallas_call x1, Pallas kernels, call1(): pl.pallas_call(functools.partial(k1, g, dv, count), out_shape=[jax.ShapeD...  40.1 us
    pallas_call x1, Pallas kernels, call2(): pl.pallas_call(k2, out_shape=[jax.ShapeDtypeStruct((4, 512, 256), BF), ja...  13.1 us

profile of v4, /device:TPU:1, one launch (start us, length us, event | category | flops | bytes accessed | tf_op | source)
XLA Modules:
  0.0 54.0 jit_solution(7660137136164240881)
XLA Ops:
  0.6 40.1 %shard_map.59 = (f32[4,512,256]{2,1,0:T(8,128)S(1)}, bf16[4,512,512]{2,1,0:T(8,128)(2,1)S(1)}, f32[2,256,768]{2,1,0:T(8,128)S(1)}) custom-call(f32[3,4,512]{2,1,0:T(4,128)} %bitcast.1, bf16[4,512,256]{2,1,0:T(8,128)(2,1)} %sk_ref.1, s32[4,6]{1,0:T(4,128)} %pat_ref.1, s32[4,512]{1,0:T(4,128)} %ord_ref.1), custom_call_target="tpu_custom_call" | custom-call | tf_op jit(solution)/shard_map/pallas_call | solution.py:203
  40.8 13.1 %shard_map.60 = (bf16[4,512,256]{2,1,0:T(8,128)(2,1)}, f32[4,256,256]{2,1,0:T(8,128)}) custom-call(f32[4,512,256]{2,1,0:T(8,128)S(1)} %get-tuple-element.5.s_ref, bf16[4,512,512]{2,1,0:T(8,128)(2,1)S(1)} %get-tuple-element.6.perm_ref, f32[2,256,768]{2,1,0:T(8,128)S(1)} %get-tuple-element.7.mid_ref), custom_call_target="tpu_custom_call" | custom-call | tf_op jit(solution)/shard_map/pallas_call | solution.py:316
